TPU v7x, 128 devices: a whole 4x4x4 slice. The times are simulated.
128 devices in a mesh: hi: 8 (over z, x_lo), lo: 16 (over x_hi, y, core).
Axes of the slice: x: 4 (x_hi: 2, x_lo: 2; x = x_hi * 2 + x_lo), y: 4, z: 4, core: 2. Of those that a mesh axis runs over, the one named last changes fastest.
Arguments:
- stem: float32 [1024, 256, 1024], P(('hi', 'lo')), may hold values from -6 to 6
- first_branch: float32 [8, 1024, 1024], P(None, 'lo'), may hold values from -0.1875 to 0.1875
- second_branch: float32 [8, 1024, 1024], P(None, 'lo'), may hold values from -0.1875 to 0.1875
- assign: int32 [2], replicated, may hold values from 0 to 7
Outputs:
- contracted: float32 [1024, 256, 1024], P(('hi', 'lo'))
Inputs may be any that keep to these rules, and one draw needn't show every extreme that they name: assign[0] selects the first branch's slice, assign[1] the second's.
All inputs are finite; a program needn't handle non-finite values.
Results may differ from a plain program's by a relative error of at most 0.00007.
Values sent between devices are 32-bit elements; how exact they have to be, the bound alone decides.
A program may use at most 128 MiB of HBM per device.

v0:
```python
import jax
import jax.numpy as jnp
from jax import lax
from jax.sharding import PartitionSpec as P


def absorb_first(stem_block, first_part):
    row_count = stem_block.shape[0] * stem_block.shape[1]
    flattened = stem_block.reshape(row_count, stem_block.shape[2])

    def add_rows(accum, portion, offset):
        return jnp.dot(
            flattened, portion, precision=lax.Precision.HIGHEST, preferred_element_type=jnp.float32
        )

    zeroes = jnp.zeros((row_count, first_part.shape[1]), jnp.float32)
    result = add_rows(zeroes, lax.all_gather(first_part, "lo", axis=0, tiled=True), jnp.int32(0))
    return result.reshape(stem_block.shape[0], stem_block.shape[1], first_part.shape[1])


def absorb_second(spread, second_part):
    flattened = spread.reshape(spread.shape[0], spread.shape[1] * spread.shape[2])

    def add_rows(accum, portion, offset):
        return lax.dot_general(
            portion,
            flattened,
            (((0,), (0,)), ((), ())),
            precision=lax.Precision.HIGHEST,
            preferred_element_type=jnp.float32,
        )

    zeroes = jnp.zeros((second_part.shape[1], flattened.shape[1]), jnp.float32)
    result = add_rows(zeroes, lax.all_gather(second_part, "lo", axis=0, tiled=True), jnp.int32(0))
    return result.reshape(second_part.shape[1], spread.shape[1], spread.shape[2])


def outward_direct(stem_block):
    return lax.all_to_all(stem_block, ("hi", "lo"), split_axis=1, concat_axis=0, tiled=True)


def inward_direct(spread):
    return lax.all_to_all(spread, ("hi", "lo"), split_axis=0, concat_axis=1, tiled=True)


def body(stem, first_branch, second_branch, assign):
    first_part = lax.dynamic_index_in_dim(first_branch, assign[0], 0, keepdims=False)
    second_part = lax.dynamic_index_in_dim(second_branch, assign[1], 0, keepdims=False)
    working = stem
    working = absorb_first(working, first_part)
    spread = outward_direct(working)
    spread = absorb_second(spread, second_part)
    working = inward_direct(spread)
    return working


def solution(mesh):
    return jax.shard_map(
        body,
        mesh=mesh,
        in_specs=(P(("hi", "lo"), None, None), P(None, "lo", None), P(None, "lo", None), P()),
        out_specs=P(("hi", "lo"), None, None),
        check_vma=False,
    )
```

profile of v0, /device:TPU:33, one launch (start us, length us, event | category | flops | bytes accessed | tf_op | source)
XLA Modules:
  0.0 454.7 jit_solution(6282318040893561045)
XLA Ops:
  6.5 0.0 copy-start
  6.5 0.0 all-gather.7.cloned.1.call-start
  6.5 1.5 fusion.4
  9.9 0.0 copy-done
  10.0 0.7 constant_dynamic-slice_fusion
  10.7 0.0 all-gather.7.cloned.1.call-update
  10.7 57.3 %all-gather.7.cloned.1.call-done = f32[1,1024,1024]{2,1,0:T(8,128)} async-done(((f32[1,64,1024]{2,1,0:T(8,128)}), f32[1,1024,1024]{2,1,0:T(8,128)}) %all-gather.7.cloned.1.call-update) | async-done | bytes 4194320 | tf_op jit(solution)/shard_map/all_gather | solution.py:17
  68.0 55.7 %fusion = f32[1024,2048]{1,0:T(8,128)S(1)} fusion(f32[2048,1024]{1,0:T(8,128)} %bitcast.32, f32[1,1024,1024]{2,1,0:T(8,128)} %all-gather.7.cloned.1.call-done), kind=kOutput, calls=%fused_computation | convolution fusion | flops 25769803776 | bytes 20971520 | tf_op jit(solution)/shard_map/dot_general | solution.py:12
  123.7 7.5 %copy.19 = f32[128,8,8,256]{3,2,1,0:T(8,128)} copy(f32[128,8,8,256]{3,1,2,0:T(8,128)S(1)} %bitcast.31) | data formatting | bytes 16777216
  131.2 8.7 %copy.14 = f32[8,256,1024]{2,0,1:T(8,128)} copy(f32[8,256,1024]{1,0,2:T(8,128)} %bitcast.28) | data formatting | bytes 16777216 | tf_op jit(solution)/shard_map/reshape | solution.py:18
  139.9 6.4 %all-to-all-start = ((f32[8,256,1024]{2,0,1:T(8,128)}), f32[8,256,1024]{2,0,1:T(8,128)}, u32[]{:S(2)}, u32[]{:S(2)}) async-start(f32[8,256,1024]{2,0,1:T(8,128)} %copy.14), calls=%async_computation | async-start | bytes 16777216 | tf_op jit(solution)/shard_map/all_to_all | solution.py:39
  146.3 0.0 all-gather.5.cloned.1.call-start
  148.2 1.0 constant_dynamic-slice_fusion.1
  149.2 1.0 copy.18
  150.2 0.0 all-gather.5.cloned.1.call-update
  150.2 116.1 %all-gather.5.cloned.1.call-done = f32[1,1024,1024]{2,0,1:T(1,128)} async-done(((f32[1,64,1024]{2,0,1:T(1,128)}), f32[1,1024,1024]{2,0,1:T(1,128)}) %all-gather.5.cloned.1.call-update) | async-done | bytes 4194320 | tf_op jit(solution)/shard_map/all_gather | solution.py:34
  266.4 11.0 %copy.13 = f32[1,1024,1024]{1,2,0:T(8,128)} copy(f32[1,1024,1024]{2,0,1:T(1,128)} %all-gather.5.cloned.1.call-done) | data formatting | bytes 8388608 | tf_op jit(solution)/shard_map/all_gather | solution.py:34
  277.3 0.0 all-to-all-done
  277.3 9.2 %copy.15 = f32[2048,1024]{1,0:T(8,128)} copy(f32[2048,1024]{0,1:T(8,128)} %bitcast.10) | data formatting | bytes 16777216 | tf_op jit(solution)/shard_map/dot_general | solution.py:25
  286.6 32.0 %fusion.2 = f32[1024,2,1024]{2,0,1:T(8,128)S(1)} fusion(f32[2,1024,1024]{2,1,0:T(8,128)} %bitcast.30, f32[1,1024,1024]{1,2,0:T(8,128)} %copy.13), kind=kOutput, calls=%fused_computation.2 | convolution fusion | flops 25769803776 | bytes 20971520 | tf_op jit(solution)/shard_map/dot_general | solution.py:25
  318.6 7.9 %copy.16 = f32[1024,2,1024]{2,1,0:T(2,128)S(1)} copy(f32[1024,2,1024]{2,0,1:T(8,128)S(1)} %fusion.2) | data formatting | bytes 16777216 | tf_op jit(solution)/shard_map/dot_general | solution.py:25
  326.5 105.7 %all_to_all.33 = f32[1024,2,1024]{2,1,0:T(2,128)S(1)} all-to-all(f32[1024,2,1024]{2,1,0:T(2,128)S(1)} %copy.16), channel_id=1, replica_groups=mesh['hi'=8,'lo'=16] {'hi','lo'}, dimensions={0} | all-to-all | bytes 16777216 | tf_op jit(solution)/shard_map/all_to_all | solution.py:43
  432.2 4.8 %copy.17 = f32[8,128,2,1024]{3,2,1,0:T(2,128)} copy(f32[8,128,2,1024]{3,2,0,1:T(2,128)S(1)} %bitcast.29) | data formatting | bytes 16777216 | tf_op jit(solution)/shard_map/all_to_all | solution.py:43
  437.0 10.9 %all_to_all.30 = f32[8,256,1024]{2,1,0:T(8,128)} reshape(f32[8,128,2,1024]{3,2,1,0:T(2,128)} %copy.17) | data formatting | bytes 16777216 | tf_op jit(solution)/shard_map/all_to_all | solution.py:43
  (2 shorter events, 0.0 us)
Async XLA Ops:
  6.5 3.4 copy-start
  6.5 61.4 %all-gather.7.cloned.1.call-start = ((), (), s32[]{:S(2)}) async-start(), calls=%async_computation.3 | async-start | bytes 4456448 | tf_op jit(solution)/shard_map/all_gather | solution.py:17
  139.9 137.4 %all-to-all-start = ((f32[8,256,1024]{2,0,1:T(8,128)}), f32[8,256,1024]{2,0,1:T(8,128)}, u32[]{:S(2)}, u32[]{:S(2)}) async-start(f32[8,256,1024]{2,0,1:T(8,128)} %copy.14), calls=%async_computation | async-start | bytes 16777216 | tf_op jit(solution)/shard_map/all_to_all | solution.py:39
  146.3 120.0 %all-gather.5.cloned.1.call-start = ((), (), s32[]{:S(2)}) async-start(), calls=%async_computation.2 | async-start | bytes 4456448 | tf_op jit(solution)/shard_map/all_gather | solution.py:34
  432.2 15.7 %copy-start.1 = (f32[8,64,1024]{2,1,0:T(8,128)S(1)}, f32[8,64,1024]{2,1,0:T(8,128)}, u32[]{:S(2)}) copy-start(f32[8,64,1024]{2,1,0:T(8,128)} %param.5) | copy-start | bytes 6291460
Sparse Core Ops, SparseCore 0:
  10.8 57.1 all-gather.6
  150.3 115.9 all-gather.4
where the time goes:
time: 458 us; the launch traced here: 455 us
  waiting for transfers between devices  173 us (38%)
  blocking collectives  106 us (23%)
  matrix products  87.7 us (19%)
  local copies, waits for them, and re-layouts  64.2 us (14%)
  between operations  17.3 us (4%)
  starting transfers between devices  6.46 us (1%)
    all_gather x1, waiting for transfers between devices, absorb_second(): lax.all_gather(second_part, 'lo', axis=0, tiled=True)  116 us
    all_to_all x1, blocking collectives, inward_direct(): lax.all_to_all(spread, ('hi', 'lo'), split_axis=0, concat_axis=1, tiled=T...  106 us
    all_gather x1, waiting for transfers between devices, absorb_first(): lax.all_gather(first_part, 'lo', axis=0, tiled=True)  57.3 us
    dot_general x1, matrix products, add_rows(): jnp.dot(flattened, portion, precision=lax.Precision.HIGHEST, preferred_el...  55.7 us
    dot_general x1, matrix products, add_rows(): lax.dot_general(portion, flattened, (((0,), (0,)), ((), ())), precision=l...  32 us
    dot_general x2, local copies, waits for them, and re-layouts, add_rows(): lax.dot_general(portion, flattened, (((0,), (0,)), ((), ())), precision=l...  17.2 us
    all_to_all x2, local copies, waits for them, and re-layouts, inward_direct(): lax.all_to_all(spread, ('hi', 'lo'), split_axis=0, concat_axis=1, tiled=T...  15.7 us
    all_gather x1, local copies, waits for them, and re-layouts, absorb_second(): lax.all_gather(second_part, 'lo', axis=0, tiled=True)  11 us
  transfers between devices with their start and end apart: 3, of which 2 were waited for; matrix products, arithmetic and copies ran while one was open for 3% of the time, Pallas kernels for 0%

commit v1 on v0

v1 whole, which is shorter than its diff:
```python
import functools

import jax
import jax.numpy as jnp
from jax import lax
from jax.experimental import pallas as pl
from jax.experimental.pallas import tpu as pltpu
from jax.sharding import PartitionSpec as P

MESH = pl.DeviceIdType.MESH
F32, BF16 = jnp.float32, jnp.bfloat16
N = 128
W = 1024
R = W // N
CH = 32
A = 32
Q = 8


def split(v):
    top = v.astype(BF16)
    return top, (v - top.astype(F32)).astype(BF16)


def dot3(ah, al, bh, bl):
    d = functools.partial(jnp.dot, preferred_element_type=F32)
    return d(ah, bh) + (d(ah, bl) + d(al, bh))


def device_at(x, y, z, c):
    return z * 2 + x % 2, (x // 2) * 8 + y * 2 + c


def kernel(stem, f_piece, s_piece, home, stage, turned, spread, f_all, s_all, fh, fl, sh, sl, yh, yl,
           stage_sem, own_sem, self_sem, g_send, g_recv, x_send, x_recv, z_send, z_recv):
    hi, lo = lax.axis_index("hi"), lax.axis_index("lo")
    me = hi * 16 + lo
    x, y, z, c = (lo // 8) * 2 + hi % 2, (lo // 2) % 4, hi // 2, lo % 2
    chip = lo // 2

    def load(q, slot):
        pltpu.make_async_copy(stem.at[:, pl.ds(q * CH, CH)], stage.at[slot], stage_sem.at[slot]).start()

    def relay(q, slot):
        pltpu.make_async_copy(stage.at[slot], stage.at[slot], stage_sem.at[slot]).wait()

        def one(t, _):
            block = stage[slot, :, pl.ds(pl.multiple_of(t * 8, 8), 8), :]
            rows = pl.ds(pl.multiple_of((q * CH + t * 8) * R, 8 * R), 8 * R)
            turned[rows, :] = pltpu.einshape("jmi->mji", block).reshape(8 * R, W)
            return 0

        lax.fori_loop(0, CH // 8, one, 0)

    own_f = pltpu.make_async_copy(f_piece, f_all.at[chip, c], own_sem.at[0])
    own_s = pltpu.make_async_copy(s_piece, s_all.at[chip, c], own_sem.at[1])
    own_f.start()
    own_s.start()
    for q in range(4):
        load(q, q)

    own_f.wait()
    own_s.wait()
    barrier = pltpu.get_barrier_semaphore()

    def greet(t, _):
        p = (me + t) % N
        pl.semaphore_signal(barrier, inc=1, device_id=(p // 16, p % 16), device_id_type=MESH)
        return 0

    lax.fori_loop(1, N, greet, 0)
    for q in range(4):
        relay(q, q)
        load(q + 4, q)
    pl.semaphore_wait(barrier, N - 1)

    def remote(src, dst, send, recv, target):
        return pltpu.make_async_remote_copy(
            src_ref=src, dst_ref=dst, send_sem=send, recv_sem=recv, device_id=target, device_id_type=MESH
        )

    def group(t, _):
        gx, gy = (x + 2 * (t // 4)) % 4, (y + t % 4) % 4
        target = device_at(gx, gy, z, c)
        for n, ref in enumerate((f_all, s_all)):
            for rows in (pl.ds(0, A), pl.ds(pl.multiple_of(A + z * Q, Q), Q)):
                part = ref.at[chip, c, rows]
                remote(part, part, g_send.at[n, 0], g_recv.at[n, 0], target).start()
        return 0

    lax.fori_loop(1, 8, group, 0)

    def offset(t):
        dc, u = t // 64, t % 64
        a, b, g = u % 4, (u // 4) % 4, u // 16
        target = device_at((x + a) % 4, (y + a + b) % 4, (z + a + b + g) % 4, (c + dc) % 2)
        return target, target[0] * 16 + target[1]

    my_rows = pl.ds(pl.multiple_of(me * R, R), R)

    def send_out(h):
        def one(t, _):
            target, p = offset(t)
            src = turned.at[pl.ds(pl.multiple_of((h * N + p) * R, R), R)]
            remote(src, spread.at[h, my_rows], x_send.at[h], x_recv.at[h], target).start()
            return 0

        lax.fori_loop(1, N, one, 0)
        own = pl.ds(pl.multiple_of((h * N + me) * R, R), R)
        pltpu.make_async_copy(turned.at[own], spread.at[h, my_rows], self_sem.at[h]).start()

    def send_home(h):
        own = pl.ds(pl.multiple_of((h * N + me) * R, R), R)

        def one(t, _):
            target, p = offset(t)
            src = spread.at[h, pl.ds(pl.multiple_of(p * R, R), R)]
            remote(src, home.at[own], z_send.at[h], z_recv.at[h], target).start()
            return 0

        lax.fori_loop(1, N, one, 0)
        pltpu.make_async_copy(spread.at[h, my_rows], home.at[own], self_sem.at[2 + h]).start()

    def rows_of(count):
        return spread.at[0, pl.ds(0, count)]

    def drain(count, send=None, recv=None):
        if send is not None:
            remote(rows_of(count), rows_of(count), send, send, (hi, lo)).wait_send()
        if recv is not None:
            remote(rows_of(count), rows_of(count), recv, recv, (hi, lo)).wait_recv()

    send_out(0)
    for q in range(4, 8):
        relay(q, q - 4)

    for n, ref in enumerate((f_all, s_all)):
        drain(7 * (A + Q), recv=g_recv.at[n, 0])
        for t in range(1, 4):
            part = ref.at[:, c, pl.ds(pl.multiple_of(A + z * Q, Q), Q)]
            remote(part, part, g_send.at[n, 1], g_recv.at[n, 1], device_at(x, y, (z + t) % 4, c)).start()
    send_out(1)
    for n, ref in enumerate((f_all, s_all)):
        drain(3 * 8 * Q, recv=g_recv.at[n, 1])
        part = ref.at[:, c]
        remote(part, part, g_send.at[n, 2], g_recv.at[n, 2], device_at(x, y, z, 1 - c)).start()

    drain(512, recv=g_recv.at[0, 2])

    def prepare_f(t, _):
        rows = pl.ds(pl.multiple_of(t * 64, 64), 64)
        fh[rows, :], fl[rows, :] = split(f_all[t // 2, t % 2])
        return 0

    lax.fori_loop(0, 16, prepare_f, 0)
    drain(512, recv=g_recv.at[1, 2])

    def prepare_s(t, _):
        p, cols = t // 8, pl.ds(pl.multiple_of((t % 8) * 128, 128), 128)
        block = jnp.concatenate([s_all[p, 0, :, cols], s_all[p, 1, :, cols]], axis=0)
        to = pl.ds(pl.multiple_of(p * 128, 128), 128)
        sh[cols, to], sl[cols, to] = split(block.T)
        return 0

    lax.fori_loop(0, 64, prepare_s, 0)

    for h in range(2):
        pltpu.make_async_copy(turned.at[pl.ds(0, R)], spread.at[h, my_rows], self_sem.at[h]).wait()
        drain((N - 1) * R, recv=x_recv.at[h])

        def by_first(t, _):
            rows = pl.ds(pl.multiple_of(t * 256, 256), 256)
            ah, al = split(spread[h, rows, :])

            def tile(n, _):
                cols = pl.ds(pl.multiple_of(n * 256, 256), 256)
                yh[rows, cols], yl[rows, cols] = split(dot3(ah, al, fh[:, cols], fl[:, cols]))
                return 0

            return lax.fori_loop(0, 4, tile, 0)

        lax.fori_loop(0, 4, by_first, 0)

        def by_second(t, _):
            rows = pl.ds(pl.multiple_of((t // 4) * 256, 256), 256)
            cols = pl.ds(pl.multiple_of((t % 4) * 256, 256), 256)
            spread[h, rows, cols] = dot3(sh[rows, :], sl[rows, :], yh[:, cols], yl[:, cols])
            return 0

        lax.fori_loop(0, 16, by_second, 0)
        send_home(h)

    for n in range(2):
        drain(7 * (A + Q), send=g_send.at[n, 0])
        drain(3 * 8 * Q, send=g_send.at[n, 1])
        drain(512, send=g_send.at[n, 2])
    for h in range(2):
        drain((N - 1) * R, send=x_send.at[h])
        drain((N - 1) * R, send=z_send.at[h])
        drain((N - 1) * R, recv=z_recv.at[h])
        pltpu.make_async_copy(turned.at[pl.ds(0, R)], spread.at[h, my_rows], self_sem.at[2 + h]).wait()


def exchange(stem, f_piece, s_piece):
    dma = pltpu.SemaphoreType.DMA
    return pl.pallas_call(
        kernel,
        name="exchange",
        out_shape=jax.ShapeDtypeStruct((stem.shape[1] * R, W), F32),
        in_specs=[pl.BlockSpec(memory_space=pl.ANY)] * 3,
        out_specs=pl.BlockSpec(memory_space=pl.ANY),
        scratch_shapes=[
            pltpu.VMEM((4, R, CH, W), F32),
            pltpu.VMEM((2 * W, W), F32),
            pltpu.VMEM((2, W, W), F32),
            pltpu.VMEM((8, 2, 64, W), F32),
            pltpu.VMEM((8, 2, 64, W), F32),
        ]
        + [pltpu.VMEM((W, W), BF16)] * 6
        + [dma((4,)), dma((2,)), dma((4,)), dma((2, 3)), dma((2, 3)), dma((2,)), dma((2,)), dma((2,)), dma((2,))],
        compiler_params=pltpu.CompilerParams(
            collective_id=0, has_side_effects=True, vmem_limit_bytes=60 << 20
        ),
    )(stem, f_piece, s_piece)


def settle_kernel(z_ref, o_ref):
    for t in range(CH // 8):
        block = z_ref[pl.ds(t * 8 * R, 8 * R), :].reshape(8, R, W)
        o_ref[:, pl.ds(t * 8, 8), :] = pltpu.einshape("mlk->lmk", block)


def settle(home):
    m = home.shape[0] // R
    return pl.pallas_call(
        settle_kernel,
        name="settle",
        grid=(m // CH,),
        out_shape=jax.ShapeDtypeStruct((R, m, W), F32),
        in_specs=[pl.BlockSpec((CH * R, W), lambda q: (q, 0))],
        out_specs=pl.BlockSpec((R, CH, W), lambda q: (0, q, 0)),
    )(home)


def body(stem, first_branch, second_branch, assign):
    f_piece = lax.dynamic_index_in_dim(first_branch, assign[0], 0, keepdims=False)
    s_piece = lax.dynamic_index_in_dim(second_branch, assign[1], 0, keepdims=False)
    return settle(exchange(stem, f_piece, s_piece))


def solution(mesh):
    return jax.shard_map(
        body,
        mesh=mesh,
        in_specs=(P(("hi", "lo"), None, None), P(None, "lo", None), P(None, "lo", None), P()),
        out_specs=P(("hi", "lo"), None, None),
        check_vma=False,
    )
```

time: 458 us -> 292 us (0.64)
  Pallas kernels: 0 us -> 279 us
  waiting for transfers between devices: 173 us -> 0 us
  blocking collectives: 106 us -> 0 us
  matrix products: 87.7 us -> 0 us
  local copies, waits for them, and re-layouts: 64.2 us -> 3.21 us
  between operations: 17.3 us -> 3.86 us
  starting transfers between devices: 6.46 us -> 0 us
    pallas_call x0 -> x2, Pallas kernels: none -> 279 us  [the longest x1 270 us: exchange(): pl.pallas_call(kernel, name='exchange', out_shape=jax.ShapeDtypeStruct((s...]
    all_gather x2 -> x0, waiting for transfers between devices: 173 us -> none  [the longest x1 116 us: absorb_second(): lax.all_gather(second_part, 'lo', axis=0, tiled=True)]
    all_to_all x1 -> x0, blocking collectives: 106 us -> none  [inward_direct(): lax.all_to_all(spread, ('hi', 'lo'), split_axis=0, concat_axis=1, tiled=T...]
    dot_general x2 -> x0, matrix products: 87.7 us -> none  [the longest x1 55.7 us: add_rows(): jnp.dot(flattened, portion, precision=lax.Precision.HIGHEST, preferred_el...]
    dot_general x2 -> x0, local copies, waits for them, and re-layouts: 17.2 us -> none  [add_rows(): lax.dot_general(portion, flattened, (((0,), (0,)), ((), ())), precision=l...]
    all_to_all x2 -> x0, local copies, waits for them, and re-layouts: 15.7 us -> none  [inward_direct(): lax.all_to_all(spread, ('hi', 'lo'), split_axis=0, concat_axis=1, tiled=T...]
    all_gather x1 -> x0, local copies, waits for them, and re-layouts: 11 us -> none  [absorb_second(): lax.all_gather(second_part, 'lo', axis=0, tiled=True)]
    reshape x1 -> x0, local copies, waits for them, and re-layouts: 8.75 us -> none  [absorb_first(): result.reshape(stem_block.shape[0], stem_block.shape[1], first_part.shape...]
  transfers between devices with their start and end apart: 3 -> 0, of which waited for: 2 -> 0; matrix products, arithmetic and copies ran while one was open for 3% -> 0% of each run, Pallas kernels for 0% -> 0%
where the time goes in v1:
time: 292 us; the launch traced here: 286 us
  Pallas kernels  279 us (96%)
  between operations  3.86 us (1%)
  local copies, waits for them, and re-layouts  3.21 us (1%)
    pallas_call x1, Pallas kernels, exchange(): pl.pallas_call(kernel, name='exchange', out_shape=jax.ShapeDtypeStruct((s...  270 us
    pallas_call x1, Pallas kernels, settle(): pl.pallas_call(settle_kernel, name='settle', grid=(m // CH,), out_shape=j...  9.41 us

profile of v1, /device:TPU:33, one launch (start us, length us, event | category | flops | bytes accessed | tf_op | source)
XLA Modules:
  0.0 286.3 jit_solution(1008656378430751786)
XLA Ops:
  0.0 1.3 fusion
  5.2 1.9 dynamic-slice_bitcast_fusion
  7.1 269.8 %exchange.1.z_ref = f32[2048,1024]{1,0:T(8,128)} custom-call(f32[8,256,1024]{2,1,0:T(8,128)} %stem.1, f32[64,1024]{1,0:T(8,128)} %get-tuple-element.8.f_piece, f32[64,1024]{1,0:T(8,128)} %get-tuple-element.7.s_piece), custom_call_target="tpu_custom_call" | custom-call | tf_op jit(solution)/shard_map/exchange/pallas_call | solution.py:206
  276.8 9.4 %settle.1 = f32[8,256,1024]{2,1,0:T(8,128)} custom-call(f32[2048,1024]{1,0:T(8,128)} %exchange.1.z_ref), custom_call_target="tpu_custom_call" | custom-call | tf_op jit(solution)/shard_map/settle/pallas_call | solution.py:235

commit v2 on v1

--- a/solution.py
+++ b/solution.py
@@ -13,8 +13,6 @@
 W = 1024
 R = W // N
 CH = 32
-A = 32
-Q = 8
 
 
 def split(v):
@@ -31,12 +29,12 @@
     return z * 2 + x % 2, (x // 2) * 8 + y * 2 + c
 
 
-def kernel(stem, f_piece, s_piece, home, stage, turned, spread, f_all, s_all, fh, fl, sh, sl, yh, yl,
+def kernel(assign, stem, first, second, home, stage, turned, spread, f_all, s_all, pick, fh, fl, sh, sl, yh, yl,
            stage_sem, own_sem, self_sem, g_send, g_recv, x_send, x_recv, z_send, z_recv):
     hi, lo = lax.axis_index("hi"), lax.axis_index("lo")
     me = hi * 16 + lo
     x, y, z, c = (lo // 8) * 2 + hi % 2, (lo // 2) % 4, hi // 2, lo % 2
-    chip = lo // 2
+    xh, xl = x // 2, x % 2
 
     def load(q, slot):
         pltpu.make_async_copy(stem.at[:, pl.ds(q * CH, CH)], stage.at[slot], stage_sem.at[slot]).start()
@@ -52,23 +50,28 @@
 
         lax.fori_loop(0, CH // 8, one, 0)
 
-    own_f = pltpu.make_async_copy(f_piece, f_all.at[chip, c], own_sem.at[0])
-    own_s = pltpu.make_async_copy(s_piece, s_all.at[chip, c], own_sem.at[1])
-    own_f.start()
-    own_s.start()
+    own = [pltpu.make_async_copy(ref, pick.at[n], own_sem.at[n]) for n, ref in enumerate((first, second))]
+    for copy in own:
+        copy.start()
     for q in range(4):
         load(q, q)
 
-    own_f.wait()
-    own_s.wait()
     barrier = pltpu.get_barrier_semaphore()
 
-    def greet(t, _):
-        p = (me + t) % N
+    def greet(p):
         pl.semaphore_signal(barrier, inc=1, device_id=(p // 16, p % 16), device_id_type=MESH)
-        return 0
-
-    lax.fori_loop(1, N, greet, 0)
+
+    def greet_far(t, _):
+        greet((me + t + t // 15 + 1) % N)
+        return 0
+
+    lax.fori_loop(0, 120, greet_far, 0)
+    for copy in own:
+        copy.wait()
+    for n, ref in enumerate((f_all, s_all)):
+        ref[xh, y, c] = pick[n, assign[n]]
+    for t in range(1, 8):
+        greet((me + 16 * t) % N)
     for q in range(4):
         relay(q, q)
         load(q + 4, q)
@@ -79,16 +82,30 @@
             src_ref=src, dst_ref=dst, send_sem=send, recv_sem=recv, device_id=target, device_id_type=MESH
         )
 
-    def group(t, _):
-        gx, gy = (x + 2 * (t // 4)) % 4, (y + t % 4) % 4
-        target = device_at(gx, gy, z, c)
-        for n, ref in enumerate((f_all, s_all)):
-            for rows in (pl.ds(0, A), pl.ds(pl.multiple_of(A + z * Q, Q), Q)):
-                part = ref.at[chip, c, rows]
-                remote(part, part, g_send.at[n, 0], g_recv.at[n, 0], target).start()
-        return 0
-
-    lax.fori_loop(1, 8, group, 0)
+    by_y = pl.ds(0, 16)
+    by_z = pl.ds(pl.multiple_of(16 + 8 * z, 8), 8)
+    by_x = pl.ds(pl.multiple_of(48 + 8 * xl, 8), 8)
+
+    def pass_on(part, n, step, target):
+        remote(part, part, g_send.at[n, step], g_recv.at[n, step], target).start()
+
+    def gather_1(n, ref):
+        pass_on(ref.at[xh, y, c, by_y], n, 0, device_at(3 - x, y, z, c))
+        for t in range(1, 4):
+            pass_on(ref.at[xh, y, c, by_x], n, 0, device_at(x, (y + t) % 4, z, c))
+        for t in range(1, 8):
+            pass_on(ref.at[xh, y, c, by_z], n, 0, device_at((x + 2 * (t // 4)) % 4, (y + t) % 4, z, c))
+
+    def gather_2(n, ref):
+        drain(96, recv=g_recv.at[n, 0])
+        for t in range(1, 4):
+            pass_on(ref.at[:, :, c, by_z], n, 1, device_at(x, y, (z + t) % 4, c))
+            pass_on(ref.at[:, y, c, by_y], n, 1, device_at(x, (y + t) % 4, z, c))
+            pass_on(ref.at[xh, :, c, by_x], n, 1, device_at((x + t) % 4, y, z, c))
+
+    def gather_3(n, ref):
+        drain(384, recv=g_recv.at[n, 1])
+        pass_on(ref.at[:, :, c], n, 2, device_at(x, y, z, 1 - c))
 
     def offset(t):
         dc, u = t // 64, t % 64
@@ -130,39 +147,31 @@
         if recv is not None:
             remote(rows_of(count), rows_of(count), recv, recv, (hi, lo)).wait_recv()
 
+    gather_1(0, f_all)
+    gather_1(1, s_all)
     send_out(0)
+    gather_2(0, f_all)
+    gather_2(1, s_all)
     for q in range(4, 8):
         relay(q, q - 4)
-
-    for n, ref in enumerate((f_all, s_all)):
-        drain(7 * (A + Q), recv=g_recv.at[n, 0])
-        for t in range(1, 4):
-            part = ref.at[:, c, pl.ds(pl.multiple_of(A + z * Q, Q), Q)]
-            remote(part, part, g_send.at[n, 1], g_recv.at[n, 1], device_at(x, y, (z + t) % 4, c)).start()
+    gather_3(0, f_all)
     send_out(1)
-    for n, ref in enumerate((f_all, s_all)):
-        drain(3 * 8 * Q, recv=g_recv.at[n, 1])
-        part = ref.at[:, c]
-        remote(part, part, g_send.at[n, 2], g_recv.at[n, 2], device_at(x, y, z, 1 - c)).start()
 
     drain(512, recv=g_recv.at[0, 2])
 
     def prepare_f(t, _):
         rows = pl.ds(pl.multiple_of(t * 64, 64), 64)
-        fh[rows, :], fl[rows, :] = split(f_all[t // 2, t % 2])
+        fh[rows, :], fl[rows, :] = split(f_all[t // 8, (t // 2) % 4, t % 2])
         return 0
 
     lax.fori_loop(0, 16, prepare_f, 0)
-    drain(512, recv=g_recv.at[1, 2])
 
     def prepare_s(t, _):
         p, cols = t // 8, pl.ds(pl.multiple_of((t % 8) * 128, 128), 128)
-        block = jnp.concatenate([s_all[p, 0, :, cols], s_all[p, 1, :, cols]], axis=0)
+        block = jnp.concatenate([s_all[p // 4, p % 4, n, :, cols] for n in range(2)], axis=0)
         to = pl.ds(pl.multiple_of(p * 128, 128), 128)
         sh[cols, to], sl[cols, to] = split(block.T)
         return 0
-
-    lax.fori_loop(0, 64, prepare_s, 0)
 
     for h in range(2):
         pltpu.make_async_copy(turned.at[pl.ds(0, R)], spread.at[h, my_rows], self_sem.at[h]).wait()
@@ -180,6 +189,10 @@
             return lax.fori_loop(0, 4, tile, 0)
 
         lax.fori_loop(0, 4, by_first, 0)
+        if h == 0:
+            gather_3(1, s_all)
+            drain(512, recv=g_recv.at[1, 2])
+            lax.fori_loop(0, 64, prepare_s, 0)
 
         def by_second(t, _):
             rows = pl.ds(pl.multiple_of((t // 4) * 256, 256), 256)
@@ -191,8 +204,8 @@
         send_home(h)
 
     for n in range(2):
-        drain(7 * (A + Q), send=g_send.at[n, 0])
-        drain(3 * 8 * Q, send=g_send.at[n, 1])
+        drain(96, send=g_send.at[n, 0])
+        drain(384, send=g_send.at[n, 1])
         drain(512, send=g_send.at[n, 2])
     for h in range(2):
         drain((N - 1) * R, send=x_send.at[h])
@@ -201,33 +214,46 @@
         pltpu.make_async_copy(turned.at[pl.ds(0, R)], spread.at[h, my_rows], self_sem.at[2 + h]).wait()
 
 
-def exchange(stem, f_piece, s_piece):
+def exchange(stem, first, second, assign):
     dma = pltpu.SemaphoreType.DMA
     return pl.pallas_call(
         kernel,
         name="exchange",
-        out_shape=jax.ShapeDtypeStruct((stem.shape[1] * R, W), F32),
-        in_specs=[pl.BlockSpec(memory_space=pl.ANY)] * 3,
-        out_specs=pl.BlockSpec(memory_space=pl.ANY),
+        out_shape=pltpu.VMEM((stem.shape[1] * R, W), F32),
+        in_specs=[pl.BlockSpec(memory_space=pltpu.SMEM)] + [pl.BlockSpec(memory_space=pl.ANY)] * 3,
+        out_specs=pl.BlockSpec(memory_space=pltpu.VMEM),
         scratch_shapes=[
             pltpu.VMEM((4, R, CH, W), F32),
             pltpu.VMEM((2 * W, W), F32),
             pltpu.VMEM((2, W, W), F32),
-            pltpu.VMEM((8, 2, 64, W), F32),
-            pltpu.VMEM((8, 2, 64, W), F32),
+            pltpu.VMEM((2, 4, 2, 64, W), F32),
+            pltpu.VMEM((2, 4, 2, 64, W), F32),
+            pltpu.VMEM((2, 8, 64, W), F32),
         ]
         + [pltpu.VMEM((W, W), BF16)] * 6
         + [dma((4,)), dma((2,)), dma((4,)), dma((2, 3)), dma((2, 3)), dma((2,)), dma((2,)), dma((2,)), dma((2,))],
         compiler_params=pltpu.CompilerParams(
-            collective_id=0, has_side_effects=True, vmem_limit_bytes=60 << 20
+            collective_id=0, has_side_effects=True, vmem_limit_bytes=54 << 20
         ),
-    )(stem, f_piece, s_piece)
-
-
-def settle_kernel(z_ref, o_ref):
-    for t in range(CH // 8):
-        block = z_ref[pl.ds(t * 8 * R, 8 * R), :].reshape(8, R, W)
-        o_ref[:, pl.ds(t * 8, 8), :] = pltpu.einshape("mlk->lmk", block)
+    )(assign, stem, first, second)
+
+
+def settle_kernel(home, out, turned, sem):
+    m = home.shape[0] // R
+
+    def piece(t, slot):
+        return pltpu.make_async_copy(turned.at[slot], out.at[:, pl.ds(t * CH, CH)], sem.at[slot])
+
+    def one(t, _):
+        for u in range(CH // 8):
+            rows = pl.ds(pl.multiple_of((t * CH + u * 8) * R, 8 * R), 8 * R)
+            turned[t, :, pl.ds(u * 8, 8), :] = pltpu.einshape("mlk->lmk", home[rows, :].reshape(8, R, W))
+        piece(t, t).start()
+        return 0
+
+    lax.fori_loop(0, m // CH, one, 0)
+    for t in range(m // CH):
+        piece(t, t).wait()
 
 
 def settle(home):
@@ -235,17 +261,16 @@
     return pl.pallas_call(
         settle_kernel,
         name="settle",
-        grid=(m // CH,),
         out_shape=jax.ShapeDtypeStruct((R, m, W), F32),
-        in_specs=[pl.BlockSpec((CH * R, W), lambda q: (q, 0))],
-        out_specs=pl.BlockSpec((R, CH, W), lambda q: (0, q, 0)),
+        in_specs=[pl.BlockSpec(memory_space=pltpu.VMEM)],
+        out_specs=pl.BlockSpec(memory_space=pl.ANY),
+        scratch_shapes=[pltpu.VMEM((m // CH, R, CH, W), F32), pltpu.SemaphoreType.DMA((m // CH,))],
+        compiler_params=pltpu.CompilerParams(vmem_limit_bytes=24 << 20),
     )(home)
 
 
 def body(stem, first_branch, second_branch, assign):
-    f_piece = lax.dynamic_index_in_dim(first_branch, assign[0], 0, keepdims=False)
-    s_piece = lax.dynamic_index_in_dim(second_branch, assign[1], 0, keepdims=False)
-    return settle(exchange(stem, f_piece, s_piece))
+    return settle(exchange(stem, first_branch, second_branch, assign))
 
 
 def solution(mesh):

time: 292 us -> 251 us (0.86); the launches traced: 286 us -> 250 us
  Pallas kernels: 279 us -> 250 us
  between operations: 3.86 us -> 0.01 us
  local copies, waits for them, and re-layouts: 3.21 us -> 0 us
    pallas_call x2, Pallas kernels: 279 us -> 250 us  [the longest x1 247 us: exchange(): pl.pallas_call(kernel, name='exchange', out_shape=pltpu.VMEM((stem.shape[...]
where the time goes in v2:
time: 251 us; the launch traced here: 250 us
  Pallas kernels  250 us (100%)
    pallas_call x1, Pallas kernels, exchange(): pl.pallas_call(kernel, name='exchange', out_shape=pltpu.VMEM((stem.shape[...  247 us

profile of v2, /device:TPU:33, one launch (start us, length us, event | category | flops | bytes accessed | tf_op | source)
XLA Modules:
  0.0 250.4 jit_solution(742980819771059330)
XLA Ops:
  0.0 246.8 %exchange.1.home = f32[2048,1024]{1,0:T(8,128)S(1)} custom-call(s32[2]{0:T(128)} %assign.1, f32[8,256,1024]{2,1,0:T(8,128)} %stem.1, f32[8,64,1024]{2,1,0:T(8,128)} %first.1, f32[8,64,1024]{2,1,0:T(8,128)} %second.1), custom_call_target="tpu_custom_call" | custom-call | tf_op jit(solution)/shard_map/exchange/pallas_call | solution.py:219
  246.8 3.6 %settle.1 = f32[8,256,1024]{2,1,0:T(8,128)} custom-call(f32[2048,1024]{1,0:T(8,128)S(1)} %exchange.1.home), custom_call_target="tpu_custom_call" | custom-call | tf_op jit(solution)/shard_map/settle/pallas_call | solution.py:261

commit v3 on v2

--- a/solution.py
+++ b/solution.py
@@ -12,7 +12,16 @@
 N = 128
 W = 1024
 R = W // N
+EARLY = 33
 CH = 32
+
+
+def div(a, b):
+    return lax.div(a, jnp.int32(b))
+
+
+def rem(a, b):
+    return lax.rem(a, jnp.int32(b))
 
 
 def split(v):
@@ -26,7 +35,7 @@
 
 
 def device_at(x, y, z, c):
-    return z * 2 + x % 2, (x // 2) * 8 + y * 2 + c
+    return z * 2 + rem(x, 2), div(x, 2) * 8 + y * 2 + c
 
 
 def kernel(assign, stem, first, second, home, stage, turned, spread, f_all, s_all, pick, fh, fl, sh, sl, yh, yl,
@@ -59,19 +68,21 @@
     barrier = pltpu.get_barrier_semaphore()
 
     def greet(p):
-        pl.semaphore_signal(barrier, inc=1, device_id=(p // 16, p % 16), device_id_type=MESH)
+        pl.semaphore_signal(barrier, inc=1, device_id=(div(p, 16), rem(p, 16)), device_id_type=MESH)
 
     def greet_far(t, _):
-        greet((me + t + t // 15 + 1) % N)
-        return 0
-
-    lax.fori_loop(0, 120, greet_far, 0)
+        other = rem(hi + t, 8)
+        for k in range(1, 16):
+            pl.semaphore_signal(barrier, inc=1, device_id=(other, rem(lo + k, 16)), device_id_type=MESH)
+        return 0
+
+    lax.fori_loop(0, 8, greet_far, 0)
     for copy in own:
         copy.wait()
     for n, ref in enumerate((f_all, s_all)):
         ref[xh, y, c] = pick[n, assign[n]]
     for t in range(1, 8):
-        greet((me + 16 * t) % N)
+        greet(rem(me + 16 * t, N))
     for q in range(4):
         relay(q, q)
         load(q + 4, q)
@@ -108,21 +119,23 @@
         pass_on(ref.at[:, :, c], n, 2, device_at(x, y, z, 1 - c))
 
     def offset(t):
-        dc, u = t // 64, t % 64
-        a, b, g = u % 4, (u // 4) % 4, u // 16
-        target = device_at((x + a) % 4, (y + a + b) % 4, (z + a + b + g) % 4, (c + dc) % 2)
+        dc, u = div(t, 64), rem(t, 64)
+        a, b, g = rem(u, 4), rem(div(u, 4), 4), div(u, 16)
+        target = device_at(rem(x + a, 4), rem(y + a + b, 4), rem(z + a + b + g, 4), rem(c + dc, 2))
         return target, target[0] * 16 + target[1]
 
     my_rows = pl.ds(pl.multiple_of(me * R, R), R)
 
-    def send_out(h):
+    def send_out(h, begin, end):
         def one(t, _):
             target, p = offset(t)
             src = turned.at[pl.ds(pl.multiple_of((h * N + p) * R, R), R)]
             remote(src, spread.at[h, my_rows], x_send.at[h], x_recv.at[h], target).start()
             return 0
 
-        lax.fori_loop(1, N, one, 0)
+        lax.fori_loop(begin, end, one, 0)
+        if end < N:
+            return
         own = pl.ds(pl.multiple_of((h * N + me) * R, R), R)
         pltpu.make_async_copy(turned.at[own], spread.at[h, my_rows], self_sem.at[h]).start()
 
@@ -149,13 +162,15 @@
 
     gather_1(0, f_all)
     gather_1(1, s_all)
-    send_out(0)
+    send_out(0, 1, N)
     gather_2(0, f_all)
     gather_2(1, s_all)
     for q in range(4, 8):
         relay(q, q - 4)
     gather_3(0, f_all)
-    send_out(1)
+    send_out(1, 1, EARLY)
+    gather_3(1, s_all)
+    send_out(1, EARLY, N)
 
     drain(512, recv=g_recv.at[0, 2])
 
@@ -190,7 +205,6 @@
 
         lax.fori_loop(0, 4, by_first, 0)
         if h == 0:
-            gather_3(1, s_all)
             drain(512, recv=g_recv.at[1, 2])
             lax.fori_loop(0, 64, prepare_s, 0)
 

time: 251 us -> 231 us (0.920)
  Pallas kernels: 250 us -> 231 us
    pallas_call x1, Pallas kernels: 247 us -> 228 us  [exchange(): pl.pallas_call(kernel, name='exchange', out_shape=pltpu.VMEM((stem.shape[...]
where the time goes in v3:
time: 231 us
  Pallas kernels  231 us (100%)
    pallas_call x1, Pallas kernels, exchange(): pl.pallas_call(kernel, name='exchange', out_shape=pltpu.VMEM((stem.shape[...  228 us

profile of v3, /device:TPU:33, one launch (start us, length us, event | category | flops | bytes accessed | tf_op | source)
XLA Modules:
  0.0 231.3 jit_solution(5364434834670014956)
XLA Ops:
  0.0 227.7 %exchange.1.home = f32[2048,1024]{1,0:T(8,128)S(1)} custom-call(s32[2]{0:T(128)} %assign.1, f32[8,256,1024]{2,1,0:T(8,128)} %stem.1, f32[8,64,1024]{2,1,0:T(8,128)} %first.1, f32[8,64,1024]{2,1,0:T(8,128)} %second.1), custom_call_target="tpu_custom_call" | custom-call | tf_op jit(solution)/shard_map/exchange/pallas_call | solution.py:233
  227.7 3.6 %settle.1 = f32[8,256,1024]{2,1,0:T(8,128)} custom-call(f32[2048,1024]{1,0:T(8,128)S(1)} %exchange.1.home), custom_call_target="tpu_custom_call" | custom-call | tf_op jit(solution)/shard_map/settle/pallas_call | solution.py:275

commit v4 on v3

--- a/solution.py
+++ b/solution.py
@@ -12,6 +12,7 @@
 N = 128
 W = 1024
 R = W // N
+FIRST = 64
 EARLY = 33
 CH = 32
 
@@ -67,22 +68,22 @@
 
     barrier = pltpu.get_barrier_semaphore()
 
-    def greet(p):
-        pl.semaphore_signal(barrier, inc=1, device_id=(div(p, 16), rem(p, 16)), device_id_type=MESH)
-
-    def greet_far(t, _):
+    def greet(t, _):
         other = rem(hi + t, 8)
         for k in range(1, 16):
             pl.semaphore_signal(barrier, inc=1, device_id=(other, rem(lo + k, 16)), device_id_type=MESH)
+
+        @pl.when(t > 0)
+        def _():
+            pl.semaphore_signal(barrier, inc=1, device_id=(other, lo), device_id_type=MESH)
+
         return 0
 
-    lax.fori_loop(0, 8, greet_far, 0)
+    lax.fori_loop(0, 8, greet, 0)
     for copy in own:
         copy.wait()
     for n, ref in enumerate((f_all, s_all)):
         ref[xh, y, c] = pick[n, assign[n]]
-    for t in range(1, 8):
-        greet(rem(me + 16 * t, N))
     for q in range(4):
         relay(q, q)
         load(q + 4, q)
@@ -93,30 +94,70 @@
             src_ref=src, dst_ref=dst, send_sem=send, recv_sem=recv, device_id=target, device_id_type=MESH
         )
 
-    by_y = pl.ds(0, 16)
-    by_z = pl.ds(pl.multiple_of(16 + 8 * z, 8), 8)
-    by_x = pl.ds(pl.multiple_of(48 + 8 * xl, 8), 8)
+    up = [rem(v + 1, 4) for v in (x, y, z)]
+    down = [rem(v + 3, 4) for v in (x, y, z)]
+    chip = xh * 4 + y
+
+    def y_rows(half):
+        return pl.ds(8 * half, 8)
+
+    def z_rows(layer):
+        return pl.ds(pl.multiple_of(16 + 8 * layer, 8), 8)
+
+    def x_rows(column):
+        return pl.ds(pl.multiple_of(48 + 8 * rem(column, 2), 8), 8)
 
     def pass_on(part, n, step, target):
         remote(part, part, g_send.at[n, step], g_recv.at[n, step], target).start()
 
     def gather_1(n, ref):
-        pass_on(ref.at[xh, y, c, by_y], n, 0, device_at(3 - x, y, z, c))
+        for half in range(2):
+            pass_on(ref.at[xh, y, c, y_rows(half)], n, 0, device_at(3 - x, y, z, c))
         for t in range(1, 4):
-            pass_on(ref.at[xh, y, c, by_x], n, 0, device_at(x, (y + t) % 4, z, c))
+            pass_on(ref.at[xh, y, c, x_rows(x)], n, 0, device_at(x, rem(y + t, 4), z, c))
         for t in range(1, 8):
-            pass_on(ref.at[xh, y, c, by_z], n, 0, device_at((x + 2 * (t // 4)) % 4, (y + t) % 4, z, c))
+            target = device_at(rem(x + 2 * (t // 4), 4), rem(y + t, 4), z, c)
+            pass_on(ref.at[xh, y, c, z_rows(z)], n, 0, target)
 
     def gather_2(n, ref):
         drain(96, recv=g_recv.at[n, 0])
-        for t in range(1, 4):
-            pass_on(ref.at[:, :, c, by_z], n, 1, device_at(x, y, (z + t) % 4, c))
-            pass_on(ref.at[:, y, c, by_y], n, 1, device_at(x, (y + t) % 4, z, c))
-            pass_on(ref.at[xh, :, c, by_x], n, 1, device_at((x + t) % 4, y, z, c))
+        for side in (up, down):
+            def along_z(t, _):
+                other = rem(chip + t, 8)
+                pass_on(ref.at[div(other, 4), rem(other, 4), c, z_rows(z)], n, 1, device_at(x, y, side[2], c))
+                return 0
+
+            lax.fori_loop(1, 8, along_z, 0)
+            for e in range(2):
+                for half in range(2):
+                    pass_on(ref.at[e, y, c, y_rows(half)], n, 1, device_at(x, side[1], z, c))
+            for t in range(1, 4):
+                pass_on(ref.at[xh, rem(y + t, 4), c, x_rows(x)], n, 1, device_at(side[0], y, z, c))
+
+            @pl.when(div(side[0], 2) != xh)
+            def _():
+                pass_on(ref.at[xh, y, c, x_rows(x)], n, 1, device_at(side[0], y, z, c))
 
     def gather_3(n, ref):
-        drain(384, recv=g_recv.at[n, 1])
-        pass_on(ref.at[:, :, c], n, 2, device_at(x, y, z, 1 - c))
+        drain(232, recv=g_recv.at[n, 1])
+
+        def along_z(t, _):
+            other = rem(chip + t, 8)
+            e = div(other, 4)
+            back, forth = rem(z + 3 + 2 * e, 4), rem(z + 1 + 2 * e, 4)
+            pass_on(ref.at[e, rem(other, 4), c, z_rows(back)], n, 2, device_at(x, y, forth, c))
+            return 0
+
+        lax.fori_loop(1, 8, along_z, 0)
+        for e, back, forth in ((0, down, up), (1, up, down)):
+            for half in range(2):
+                pass_on(ref.at[e, back[1], c, y_rows(half)], n, 2, device_at(x, forth[1], z, c))
+                part = ref.at[div(back[0], 2), 2 * e + half, c, x_rows(back[0])]
+                pass_on(part, n, 2, device_at(forth[0], y, z, c))
+
+    def gather_4(n, ref):
+        drain(120, recv=g_recv.at[n, 2])
+        pass_on(ref.at[:, :, c], n, 3, device_at(x, y, z, 1 - c))
 
     def offset(t):
         dc, u = div(t, 64), rem(t, 64)
@@ -162,17 +203,20 @@
 
     gather_1(0, f_all)
     gather_1(1, s_all)
-    send_out(0, 1, N)
+    send_out(0, 1, FIRST)
     gather_2(0, f_all)
     gather_2(1, s_all)
+    send_out(0, FIRST, N)
     for q in range(4, 8):
         relay(q, q - 4)
     gather_3(0, f_all)
+    gather_3(1, s_all)
     send_out(1, 1, EARLY)
-    gather_3(1, s_all)
+    gather_4(0, f_all)
+    gather_4(1, s_all)
     send_out(1, EARLY, N)
 
-    drain(512, recv=g_recv.at[0, 2])
+    drain(512, recv=g_recv.at[0, 3])
 
     def prepare_f(t, _):
         rows = pl.ds(pl.multiple_of(t * 64, 64), 64)
@@ -205,7 +249,7 @@
 
         lax.fori_loop(0, 4, by_first, 0)
         if h == 0:
-            drain(512, recv=g_recv.at[1, 2])
+            drain(512, recv=g_recv.at[1, 3])
             lax.fori_loop(0, 64, prepare_s, 0)
 
         def by_second(t, _):
@@ -219,8 +263,9 @@
 
     for n in range(2):
         drain(96, send=g_send.at[n, 0])
-        drain(384, send=g_send.at[n, 1])
-        drain(512, send=g_send.at[n, 2])
+        drain(232, send=g_send.at[n, 1])
+        drain(120, send=g_send.at[n, 2])
+        drain(512, send=g_send.at[n, 3])
     for h in range(2):
         drain((N - 1) * R, send=x_send.at[h])
         drain((N - 1) * R, send=z_send.at[h])
@@ -245,7 +290,7 @@
             pltpu.VMEM((2, 8, 64, W), F32),
         ]
         + [pltpu.VMEM((W, W), BF16)] * 6
-        + [dma((4,)), dma((2,)), dma((4,)), dma((2, 3)), dma((2, 3)), dma((2,)), dma((2,)), dma((2,)), dma((2,))],
+        + [dma((4,)), dma((2,)), dma((4,)), dma((2, 4)), dma((2, 4)), dma((2,)), dma((2,)), dma((2,)), dma((2,))],
         compiler_params=pltpu.CompilerParams(
             collective_id=0, has_side_effects=True, vmem_limit_bytes=54 << 20
         ),

time: 231 us -> 225 us (0.974)
  Pallas kernels: 231 us -> 224 us
    pallas_call x1, Pallas kernels: 228 us -> 221 us  [exchange(): pl.pallas_call(kernel, name='exchange', out_shape=pltpu.VMEM((stem.shape[...]
where the time goes in v4:
time: 225 us
  Pallas kernels  224 us (100%)
    pallas_call x1, Pallas kernels, exchange(): pl.pallas_call(kernel, name='exchange', out_shape=pltpu.VMEM((stem.shape[...  221 us

profile of v4, /device:TPU:33, one launch (start us, length us, event | category | flops | bytes accessed | tf_op | source)
XLA Modules:
  0.0 224.5 jit_solution(15578963589201808300)
XLA Ops:
  0.0 220.9 %exchange.1.home = f32[2048,1024]{1,0:T(8,128)S(1)} custom-call(s32[2]{0:T(128)} %assign.1, f32[8,256,1024]{2,1,0:T(8,128)} %stem.1, f32[8,64,1024]{2,1,0:T(8,128)} %first.1, f32[8,64,1024]{2,1,0:T(8,128)} %second.1), custom_call_target="tpu_custom_call" | custom-call | tf_op jit(solution)/shard_map/exchange/pallas_call | solution.py:278
  220.9 3.6 %settle.1 = f32[8,256,1024]{2,1,0:T(8,128)} custom-call(f32[2048,1024]{1,0:T(8,128)S(1)} %exchange.1.home), custom_call_target="tpu_custom_call" | custom-call | tf_op jit(solution)/shard_map/settle/pallas_call | solution.py:320
